TPU v7x, 256 devices: a whole 4x4x8 slice. The times are simulated.
256 devices in a mesh: slab: 64 (over x_lo, y, z), subj: 2 (over core), tm: 2 (over x_hi).
Axes of the slice: x: 4 (x_hi: 2, x_lo: 2; x = x_hi * 2 + x_lo), y: 4, z: 8, core: 2. Of those that a mesh axis runs over, the one named last changes fastest.
Arguments:
- subject_data: bfloat16 [2, 128, 128, 2048], P('subj', 'slab', None, 'tm'), may hold values from -8 to 8
- template: bfloat16 [128, 128, 2048], P('slab', None, 'tm'), may hold values from -8 to 8
- neighbours: int32 [128, 27], P('slab'), may hold values from 0 to 127, as said below
- valid: int32 [128, 27], P('slab'), may hold values from 0 to 1, as said below
Outputs:
- new_template: bfloat16 [128, 128, 2048], P('slab', None, 'tm')
Inputs may be any that keep to these rules, and one draw needn't show every extreme that they name: `neighbours`: slots 9 l to 9 l + 8 of block b name blocks of the slab of b shifted by l - 1 (slabs hold 2 consecutive blocks); where that slab doesn't exist they name b itself. Slot 13 names b itself. `valid`: slot 13 is always 1; slots whose slab doesn't exist are 0.
All inputs are finite; a program needn't handle non-finite values.
Results may differ from a plain program's by a relative error of at most 0.007.
Values may be sent and summed in bfloat16 or wider, within the bound.
A program may use at most 64 MiB of HBM per device.

v0:
```python
import jax
import jax.numpy as jnp
from jax import lax
from jax.sharding import PartitionSpec as P

ITERS = 3


def from_everyone(x, axis):
    size = lax.axis_size(axis)
    return lax.all_to_all(jnp.broadcast_to(x[None], (size, *x.shape)), axis, 0, 0, tiled=True)


def over_copies(x, axis):
    everything = from_everyone(x, axis)
    return jnp.sum(everything, axis=0)


def laid_out(pieces, dim):
    pieces = jnp.moveaxis(pieces, 0, dim)
    lengths = pieces.shape
    return pieces.reshape(*lengths[:dim], lengths[dim] * lengths[dim + 1], *lengths[dim + 2 :])


def gather_directly(x, axis, dim):
    return laid_out(from_everyone(x, axis), dim)


def with_halo(cells, sides, width):
    for axis, dim in sides:
        count = lax.axis_size(axis)
        ends = count - 1
        head = lax.slice_in_dim(cells, 0, width, axis=dim)
        tail = lax.slice_in_dim(cells, cells.shape[dim] - width, cells.shape[dim], axis=dim)
        cells = jnp.concatenate(
            [
                lax.ppermute(tail, axis, [(i, (i + 1) % count) for i in range(ends)]),
                cells,
                lax.ppermute(head, axis, [((i + 1) % count, i) for i in range(ends)]),
            ],
            axis=dim,
        )
    return cells


def split_up(x, dim, size):
    before, after = (x.shape[:dim], x.shape[dim + 1 :])
    return jnp.moveaxis(x.reshape(*before, size, -1, *after), dim, 0)


def edges_of(length, count):
    unit = 8 if length >= 8 * count else 1
    return [length // unit * k // count * unit for k in range(1, count)]


def exchange_in_pieces(x, axis, pieces, split_dim, concat_dim):
    blocks = split_up(x, split_dim, lax.axis_size(axis))
    cut = max(range(1, max(2, blocks.ndim - 1)), key=lambda d: blocks.shape[d])
    gathered = []
    for piece in jnp.split(blocks, edges_of(blocks.shape[cut], pieces), axis=cut):
        if piece.size:
            gathered.append(lax.all_to_all(piece, axis, split_axis=0, concat_axis=0, tiled=True))
    return laid_out(jnp.concatenate(gathered, axis=cut), concat_dim)


def balance(cross, row_norm, col_norm, mask):
    width = cross.shape[-1]
    logits = cross * row_norm[None, :, None, None] * col_norm[:, None, :, :] / 0.03
    masked = mask[None, None, :, None]
    kernel = jnp.exp(logits) * masked
    target = masked / (width * jnp.sum(mask))
    filler = 1.0 - masked
    col_weight = jnp.ones((cross.shape[0], 1, cross.shape[2], width), jnp.float32)
    for step in range(ITERS):
        row_weight = 1.0 / width / jnp.sum(kernel * col_weight, axis=(2, 3), keepdims=True)
        col_weight = target / (jnp.sum(kernel * row_weight, axis=1, keepdims=True) + filler)
    flow = kernel * col_weight
    return (flow / jnp.sum(flow, axis=(2, 3), keepdims=True)).astype(jnp.bfloat16)


def square_sum(values):
    return jnp.einsum("...t,...t->...", values, values, preferred_element_type=jnp.float32)


def slot_cross(tmpl_block, extended, slots):
    whole = jnp.einsum("it,sejt->siej", tmpl_block, extended, preferred_element_type=jnp.float32)
    return jnp.take(whole, slots, axis=2)


def project(plan, extended, slots):
    places = (slots[:, None] == jnp.arange(extended.shape[1], dtype=jnp.int32)[None, :]).astype(
        jnp.float32
    )
    folded = jnp.einsum(
        "sikj,ke->siej", plan.astype(jnp.float32), places, precision=lax.Precision.HIGHEST
    )
    upper = folded.astype(jnp.bfloat16)
    lower = (folded - upper.astype(jnp.float32)).astype(jnp.bfloat16)
    total = jnp.einsum("siej,sejt->it", upper, extended, preferred_element_type=jnp.float32)
    return total + jnp.einsum("siej,sejt->it", lower, extended, preferred_element_type=jnp.float32)


def subject_mean(moved, count):
    total = over_copies(moved, "subj")
    return (total / count).astype(jnp.bfloat16)


def on_device(subject_data, template, neighbours, valid):
    blocks_here = template.shape[0]
    share = blocks_here // lax.axis_size("tm")
    subjects_all = subject_data.shape[0] * lax.axis_size("subj")
    offsets = neighbours - (lax.axis_index("slab") - 1) * blocks_here
    mask_all = valid.astype(jnp.float32)
    first = lax.axis_index("tm") * share
    my_offsets = lax.dynamic_slice_in_dim(offsets, first, share, 0)
    my_mask = lax.dynamic_slice_in_dim(mask_all, first, share, 0)
    full_time = gather_directly(subject_data, "tm", 3)
    extended = with_halo(full_time, (("slab", 1),), blocks_here)
    mine = lax.all_to_all(template, "tm", split_axis=0, concat_axis=2, tiled=True)
    col_norm = lax.rsqrt(square_sum(extended) + 1e-06)
    row_norm = lax.rsqrt(square_sum(mine) + 1e-06)

    def one_block(inputs):
        tmpl_block, scale_rows, slots, mask = inputs
        cross = slot_cross(tmpl_block, extended, slots)
        plan = balance(cross, scale_rows, jnp.take(col_norm, slots, axis=1), mask)
        return project(plan, extended, slots)

    moved = lax.map(one_block, (mine, row_norm, my_offsets, my_mask))
    averaged = subject_mean(moved, subjects_all)
    return exchange_in_pieces(averaged, "tm", 2, 2, 0)


def solution(mesh):
    placed = (
        P("subj", "slab", None, "tm"),
        P("slab", None, "tm"),
        P("slab", None),
        P("slab", None),
    )
    return jax.shard_map(
        on_device, mesh=mesh, in_specs=placed, out_specs=P("slab", None, "tm"), check_vma=False
    )
```

profile of v0, /device:TPU:2, one launch (start us, length us, event | category | flops | bytes accessed | tf_op | source)
XLA Modules:
  0.0 117.3 jit_solution(14926200425164752471)
XLA Ops:
  0.0 2.2 %broadcast_in_dim.73 = bf16[2,1,2,128,1024]{4,3,2,1,0:T(8,128)(2,1)} broadcast(bf16[2,128,1024]{2,1,0:T(8,128)(2,1)} %bitcast.117), dimensions={2,3,4} | broadcast | bytes 1572864 | tf_op jit(solution)/shard_map/broadcast_in_dim | solution.py:11
  2.2 3.6 %all-to-all-start = ((bf16[2,1,2,128,1024]{4,3,2,1,0:T(8,128)(2,1)}), bf16[2,1,2,128,1024]{4,3,2,1,0:T(8,128)(2,1)S(1)}, u32[]{:S(2)}, u32[]{:S(2)}) async-start(bf16[2,1,2,128,1024]{4,3,2,1,0:T(8,128)(2,1)} %broadcast_in_dim.73), calls=%async_computation | async-start | bytes 2097152 | tf_op jit(solution)/shard_map/all_to_all | solution.py:11
  5.7 0.0 copy-start
  5.8 0.0 copy-start.1
  5.8 15.3 %all-to-all-done = bf16[2,1,2,128,1024]{4,3,2,1,0:T(8,128)(2,1)S(1)} async-done(((bf16[2,1,2,128,1024]{4,3,2,1,0:T(8,128)(2,1)}), bf16[2,1,2,128,1024]{4,3,2,1,0:T(8,128)(2,1)S(1)}, u32[]{:S(2)}, u32[]{:S(2)}) %all-to-all-start) | async-done | bytes 1048608 | tf_op jit(solution)/shard_map/all_to_all | solution.py:11
  21.1 3.5 %all-to-all-start.1 = ((bf16[2,128,1024]{2,1,0:T(8,128)(2,1)}), bf16[2,128,1024]{2,1,0:T(8,128)(2,1)S(1)}, u32[]{:S(2)}, u32[]{:S(2)}) async-start(bf16[2,128,1024]{2,1,0:T(8,128)(2,1)} %param.5), calls=%async_computation.1 | async-start | bytes 1048576 | tf_op jit(solution)/shard_map/all_to_all | solution.py:119
  24.6 0.1 copy.37
  24.7 10.6 %collective-permute-start.1 = (bf16[1,2,128,2048]{3,2,1,0:T(8,128)(2,1)S(1)}, bf16[1,2,128,2048]{3,2,1,0:T(8,128)(2,1)}, u32[]{:S(2)}, u32[]{:S(2)}) collective-permute-start(bf16[1,2,128,2048]{3,2,1,0:T(8,128)(2,1)S(1)} %bitcast.108), channel_id=1, source_target_pairs={{4,0},{8,4},{12,8},{16,12},{20,16},{24,20},{28,24},{32,28},{36,32}... | collective-permute-start | bytes 3145736 | tf_op jit(solution)/shard_map/ppermute | solution.py:39
  35.3 1.9 %collective-permute-start = (bf16[1,2,128,2048]{3,2,1,0:T(8,128)(2,1)S(1)}, bf16[1,2,128,2048]{3,2,1,0:T(8,128)(2,1)}, u32[]{:S(2)}, u32[]{:S(2)}) collective-permute-start(bf16[1,2,128,2048]{3,2,1,0:T(8,128)(2,1)S(1)} %bitcast.109), channel_id=1, source_target_pairs={{0,4},{4,8},{8,12},{12,16},{16,20},{20,24},{24,28},{28,32},{32,36}... | collective-permute-start | bytes 3145736 | tf_op jit(solution)/shard_map/ppermute | solution.py:37
  37.3 0.6 fusion.24
  38.7 0.5 copy.22
  39.2 0.4 reshape.364
  39.6 0.1 copy.38
  39.7 0.2 fusion.15
  39.9 16.6 %collective-permute-done.1 = bf16[1,2,128,2048]{3,2,1,0:T(8,128)(2,1)} collective-permute-done((bf16[1,2,128,2048]{3,2,1,0:T(8,128)(2,1)S(1)}, bf16[1,2,128,2048]{3,2,1,0:T(8,128)(2,1)}, u32[]{:S(2)}, u32[]{:S(2)}) %collective-permute-start.1) | collective-permute-done | bytes 1048608 | tf_op jit(solution)/shard_map/ppermute | solution.py:39
  56.5 8.4 %collective-permute-done = bf16[1,2,128,2048]{3,2,1,0:T(8,128)(2,1)} collective-permute-done((bf16[1,2,128,2048]{3,2,1,0:T(8,128)(2,1)S(1)}, bf16[1,2,128,2048]{3,2,1,0:T(8,128)(2,1)}, u32[]{:S(2)}, u32[]{:S(2)}) %collective-permute-start) | collective-permute-done | bytes 1048608 | tf_op jit(solution)/shard_map/ppermute | solution.py:37
  65.0 2.0 %fusion = f32[6,128]{1,0:T(8,128)S(1)} fusion(bf16[1,2,128,2048]{3,2,1,0:T(8,128)(2,1)} %collective-permute-done.1, bf16[1,2,128,2048]{3,2,1,0:T(8,128)(2,1)S(1)} %bitcast.110, bf16[1,2,128,2048]{3,2,1,0:T(8,128)(2,1)} %collective-permute-done), kind=kLoop, calls=%fused_computation.3 | loop fusion | flops 7863552 | bytes 3148800 | tf_op jit(solution)/shard_map/...t,...t->.../dot_general | solution.py:82
  67.0 0.6 gather_fusion.1
  67.5 2.5 %convolution_bitcast_fusion.3 = f32[128,6,128]{0,2,1:T(8,128)S(1)} fusion(bf16[128,2048,1]{1,0,2:T(8,128)(2,1)S(1)} %reshape.364, bf16[1,2,128,2048]{3,2,1,0:T(8,128)(2,1)} %collective-permute-done.1, bf16[1,2,128,2048]{3,2,1,0:T(8,128)(2,1)S(1)} %bitcast.111, bf16[1,2,128,2048]{3,2,1,0:T(8,128)(2,1)} %collective-permute-done), kind=kOutput, calls=%fused_computation.30 | convolution fusion | flops 405798912 | bytes 4063232 | tf_op jit(solution)/shard_map/while/body/eval_jaxpr/it,sejt->siej/dot_general | solution.py:86
  70.1 0.7 gather_fusion
  70.7 0.1 broadcast_select_fusion
  70.8 0.8 fusion.26
  71.6 1.4 %multiply_reduce_fusion.5 = f32[27,128]{1,0:T(8,128)S(1)} fusion(f32[128]{0:T(128)S(1)} %broadcast_divide_fusion.2, f32[27]{0:T(128)S(1)} %get-tuple-element.20, f32[27,128]{1,0:T(8,128)S(1)} %broadcast_select_fusion, f32[128]{0:T(128)S(1)} %add_rsqrt_fusion.1, f32[27,128,128]{1,2,0:T(8,128)S(1)} %gather_fusion, pred[27]{0:T(512)(128)(4,1)S(1)} %get-tuple-element.21), kind=kLoop, calls=%fused_computation.27 | loop fusion | flops 3093120 | bytes 1798279 | tf_op jit(solution)/shard_map/while/body/eval_jaxpr/reduce_sum | solution.py:76
  73.0 0.1 add_divide_fusion.2
  73.1 1.3 %multiply_reduce_fusion.4 = f32[128]{0:T(128)S(1)} fusion(f32[27,128]{1,0:T(8,128)S(1)} %add_divide_fusion.2, f32[27]{0:T(128)S(1)} %get-tuple-element.20, f32[27,128]{1,0:T(8,128)S(1)} %broadcast_select_fusion, f32[128]{0:T(128)S(1)} %add_rsqrt_fusion.1, f32[27,128,128]{1,2,0:T(8,128)S(1)} %gather_fusion, pred[27]{0:T(512)(128)(4,1)S(1)} %get-tuple-element.21), kind=kLoop, calls=%fused_computation.26 | loop fusion | flops 3096448 | bytes 1798279 | tf_op jit(solution)/shard_map/while/body/eval_jaxpr/reduce_sum | solution.py:75
  74.4 1.4 %multiply_reduce_fusion.3 = f32[27,128]{1,0:T(8,128)S(1)} fusion(f32[128]{0:T(128)S(1)} %broadcast_divide_fusion.1, f32[27]{0:T(128)S(1)} %get-tuple-element.20, f32[27,128]{1,0:T(8,128)S(1)} %broadcast_select_fusion, f32[128]{0:T(128)S(1)} %add_rsqrt_fusion.1, f32[27,128,128]{1,2,0:T(8,128)S(1)} %gather_fusion, pred[27]{0:T(512)(128)(4,1)S(1)} %get-tuple-element.21), kind=kLoop, calls=%fused_computation.25 | loop fusion | flops 3093120 | bytes 1798279 | tf_op jit(solution)/shard_map/while/body/eval_jaxpr/reduce_sum | solution.py:76
  75.8 0.1 add_divide_fusion.1
  75.9 1.3 %multiply_reduce_fusion.2 = f32[128]{0:T(128)S(1)} fusion(f32[27,128]{1,0:T(8,128)S(1)} %add_divide_fusion.1, f32[27]{0:T(128)S(1)} %get-tuple-element.20, f32[27,128]{1,0:T(8,128)S(1)} %broadcast_select_fusion, f32[128]{0:T(128)S(1)} %add_rsqrt_fusion.1, f32[27,128,128]{1,2,0:T(8,128)S(1)} %gather_fusion, pred[27]{0:T(512)(128)(4,1)S(1)} %get-tuple-element.21), kind=kLoop, calls=%fused_computation.24 | loop fusion | flops 3096448 | bytes 1798279 | tf_op jit(solution)/shard_map/while/body/eval_jaxpr/reduce_sum | solution.py:75
  77.3 1.4 %multiply_reduce_fusion.1 = f32[27,128]{1,0:T(8,128)S(1)} fusion(f32[128]{0:T(128)S(1)} %broadcast_divide_fusion, f32[27]{0:T(128)S(1)} %get-tuple-element.20, f32[27,128]{1,0:T(8,128)S(1)} %broadcast_select_fusion, f32[128]{0:T(128)S(1)} %add_rsqrt_fusion.1, f32[27,128,128]{1,2,0:T(8,128)S(1)} %gather_fusion, pred[27]{0:T(512)(128)(4,1)S(1)} %get-tuple-element.21), kind=kLoop, calls=%fused_computation.23 | loop fusion | flops 3093120 | bytes 1798279 | tf_op jit(solution)/shard_map/while/body/eval_jaxpr/reduce_sum | solution.py:76
  78.6 0.1 add_divide_fusion
  78.7 1.3 %multiply_reduce_fusion = f32[128]{0:T(128)S(1)} fusion(f32[27,128]{1,0:T(8,128)S(1)} %add_divide_fusion, f32[27]{0:T(128)S(1)} %get-tuple-element.20, f32[27,128]{1,0:T(8,128)S(1)} %broadcast_select_fusion, f32[128]{0:T(128)S(1)} %add_rsqrt_fusion.1, f32[27,128,128]{1,2,0:T(8,128)S(1)} %gather_fusion, pred[27]{0:T(512)(128)(4,1)S(1)} %get-tuple-element.21), kind=kLoop, calls=%fused_computation.22 | loop fusion | flops 3096448 | bytes 1798279 | tf_op jit(solution)/shard_map/while/body/eval_jaxpr/reduce_sum | solution.py:78
  80.1 2.3 %fusion.14 = bf16[128,27,128]{0,2,1:T(8,128)(2,1)} fusion(f32[27,128,128]{1,2,0:T(8,128)S(1)} %gather_fusion, f32[128]{0:T(128)S(1)} %multiply_reduce_fusion, f32[27,128]{1,0:T(8,128)S(1)} %add_divide_fusion, f32[27]{0:T(128)S(1)} %get-tuple-element.20, f32[27,128]{1,0:T(8,128)S(1)} %broadcast_select_fusion, f32[128]{0:T(128)S(1)} %add_rsqrt_fusion.1, ...), kind=kLoop, calls=%fused_computation.28 | loop fusion | flops 3538944 | bytes 2683015 | tf_op jit(solution)/shard_map/while/body/eval_jaxpr/convert_element_type | solution.py:78
  82.4 1.9 %copy.23 = bf16[128,27,128]{2,1,0:T(8,128)(2,1)S(1)} copy(bf16[128,27,128]{0,2,1:T(8,128)(2,1)} %fusion.14) | data formatting | bytes 1769472 | tf_op jit(solution)/shard_map/while/body/eval_jaxpr/convert_element_type | solution.py:78
  84.3 0.3 convert_bitcast_fusion
  84.6 2.3 %convolution_bitcast_fusion = f32[128,2048]{1,0:T(8,128)S(1)} fusion(bf16[128,6,128]{2,1,0:T(8,128)(2,1)S(1)} %get-tuple-element.36, bf16[1,2,128,2048]{3,2,1,0:T(8,128)(2,1)} %collective-permute-done.1, bf16[1,2,128,2048]{3,2,1,0:T(8,128)(2,1)S(1)} %bitcast.112, bf16[1,2,128,2048]{3,2,1,0:T(8,128)(2,1)} %collective-permute-done), kind=kOutput, calls=%fused_computation.5 | convolution fusion | flops 405798912 | bytes 4390912 | tf_op jit(solution)/shard_map/while/body/eval_jaxpr/siej,sejt->it/dot_general | solution.py:100
  86.9 2.3 %fusion.1 = f32[128,2048]{1,0:T(8,128)S(1)} fusion(f32[128,2048]{1,0:T(8,128)S(1)} %convolution_bitcast_fusion, bf16[128,6,128]{2,1,0:T(8,128)(2,1)S(1)} %get-tuple-element.34, bf16[1,2,128,2048]{3,2,1,0:T(8,128)(2,1)} %collective-permute-done.1, bf16[1,2,128,2048]{3,2,1,0:T(8,128)(2,1)S(1)} %bitcast.113, bf16[1,2,128,2048]{3,2,1,0:T(8,128)(2,1)} %collective-permute-done), kind=kOutput, calls=%fused_computation.7 | convolution fusion | flops 406061056 | bytes 5439488 | tf_op jit(solution)/shard_map/while/body/eval_jaxpr/siej,sejt->it/dot_general | solution.py:99
  89.2 0.2 broadcast_in_dim.79
  89.4 5.4 %all_to_all.35 = f32[2,1,128,2048]{3,2,1,0:T(8,128)S(1)} all-to-all(f32[2,1,128,2048]{3,2,1,0:T(8,128)S(1)} %broadcast_in_dim.79), channel_id=1, replica_groups=mesh['slab'=64,'subj'=2,'tm'=2] {'subj'}, dimensions={0} | all-to-all | bytes 4194304 | tf_op jit(solution)/shard_map/all_to_all | solution.py:11
  94.8 0.2 reduce_sum.97
  95.1 0.1 multiply_convert_fusion
  95.1 0.3 copy.26
  95.4 0.2 fusion.29
  95.6 0.9 copy.27
  96.5 3.9 %all-to-all-start.3 = ((bf16[2,1,64,1024]{3,2,1,0:T(8,128)(2,1)}), bf16[2,1,64,1024]{3,2,1,0:T(8,128)(2,1)S(1)}, u32[]{:S(2)}, u32[]{:S(2)}) async-start(bf16[2,1,64,1024]{3,2,1,0:T(8,128)(2,1)} %copy.27), calls=%async_computation.3 | async-start | bytes 524288 | tf_op jit(solution)/shard_map/all_to_all | solution.py:62
  100.4 0.2 copy.28
  100.6 6.8 %all-to-all-done.3 = bf16[2,1,64,1024]{3,2,1,0:T(8,128)(2,1)S(1)} async-done(((bf16[2,1,64,1024]{3,2,1,0:T(8,128)(2,1)}), bf16[2,1,64,1024]{3,2,1,0:T(8,128)(2,1)S(1)}, u32[]{:S(2)}, u32[]{:S(2)}) %all-to-all-start.3) | async-done | bytes 262176 | tf_op jit(solution)/shard_map/all_to_all | solution.py:62
  107.4 9.1 %all_to_all.36 = bf16[2,1,64,1024]{3,2,1,0:T(8,128)(2,1)S(1)} all-to-all(bf16[2,1,64,1024]{3,2,1,0:T(8,128)(2,1)S(1)} %copy.28), channel_id=1, replica_groups=mesh['slab'=64,'subj'=2,'tm'=2] {'tm'}, dimensions={0} | all-to-all | bytes 524288 | tf_op jit(solution)/shard_map/all_to_all | solution.py:62
  116.4 0.8 maximum_bitcast_fusion.1
  (15 shorter events, 0.1 us)
Async XLA Ops:
  2.2 18.9 %all-to-all-start = ((bf16[2,1,2,128,1024]{4,3,2,1,0:T(8,128)(2,1)}), bf16[2,1,2,128,1024]{4,3,2,1,0:T(8,128)(2,1)S(1)}, u32[]{:S(2)}, u32[]{:S(2)}) async-start(bf16[2,1,2,128,1024]{4,3,2,1,0:T(8,128)(2,1)} %broadcast_in_dim.73), calls=%async_computation | async-start | bytes 2097152 | tf_op jit(solution)/shard_map/all_to_all | solution.py:11
  5.7 31.5 %copy-start = (s32[2,27]{1,0:T(2,128)S(1)}, s32[2,27]{1,0:T(2,128)}, u32[]{:S(2)}) copy-start(s32[2,27]{1,0:T(2,128)} %param.6) | copy-start | bytes 652
  5.8 31.5 %copy-start.1 = (s32[2,27]{1,0:T(2,128)S(1)}, s32[2,27]{1,0:T(2,128)}, u32[]{:S(2)}) copy-start(s32[2,27]{1,0:T(2,128)} %param.7) | copy-start | bytes 652
  21.1 17.6 %all-to-all-start.1 = ((bf16[2,128,1024]{2,1,0:T(8,128)(2,1)}), bf16[2,128,1024]{2,1,0:T(8,128)(2,1)S(1)}, u32[]{:S(2)}, u32[]{:S(2)}) async-start(bf16[2,128,1024]{2,1,0:T(8,128)(2,1)} %param.5), calls=%async_computation.1 | async-start | bytes 1048576 | tf_op jit(solution)/shard_map/all_to_all | solution.py:119
  24.7 31.8 %collective-permute-start.1 = (bf16[1,2,128,2048]{3,2,1,0:T(8,128)(2,1)S(1)}, bf16[1,2,128,2048]{3,2,1,0:T(8,128)(2,1)}, u32[]{:S(2)}, u32[]{:S(2)}) collective-permute-start(bf16[1,2,128,2048]{3,2,1,0:T(8,128)(2,1)S(1)} %bitcast.108), channel_id=1, source_target_pairs={{4,0},{8,4},{12,8},{16,12},{20,16},{24,20},{28,24},{32,28},{36,32}... | collective-permute-start | bytes 3145736 | tf_op jit(solution)/shard_map/ppermute | solution.py:39
  35.3 29.6 %collective-permute-start = (bf16[1,2,128,2048]{3,2,1,0:T(8,128)(2,1)S(1)}, bf16[1,2,128,2048]{3,2,1,0:T(8,128)(2,1)}, u32[]{:S(2)}, u32[]{:S(2)}) collective-permute-start(bf16[1,2,128,2048]{3,2,1,0:T(8,128)(2,1)S(1)} %bitcast.109), channel_id=1, source_target_pairs={{0,4},{4,8},{8,12},{12,16},{16,20},{20,24},{24,28},{28,32},{32,36}... | collective-permute-start | bytes 3145736 | tf_op jit(solution)/shard_map/ppermute | solution.py:37
  96.5 10.9 %all-to-all-start.3 = ((bf16[2,1,64,1024]{3,2,1,0:T(8,128)(2,1)}), bf16[2,1,64,1024]{3,2,1,0:T(8,128)(2,1)S(1)}, u32[]{:S(2)}, u32[]{:S(2)}) async-start(bf16[2,1,64,1024]{3,2,1,0:T(8,128)(2,1)} %copy.27), calls=%async_computation.3 | async-start | bytes 524288 | tf_op jit(solution)/shard_map/all_to_all | solution.py:62
where the time goes:
time: 118 us; the launch traced here: 117 us
  waiting for transfers between devices  47.2 us (40%)
  starting transfers between devices  23.5 us (20%)
  other arithmetic  15.5 us (13%)
  blocking collectives  14.5 us (12%)
  local copies, waits for them, and re-layouts  8.28 us (7%)
  matrix products  7.33 us (6%)
    ppermute x1, waiting for transfers between devices, with_halo(): lax.ppermute(head, axis, [((i + 1) % count, i) for i in range(ends)])  16.6 us
    all_to_all x1, waiting for transfers between devices, from_everyone(): lax.all_to_all(jnp.broadcast_to(x[None], (size, *x.shape)), axis, 0, 0, t...  15.3 us
    ppermute x1, starting transfers between devices, with_halo(): lax.ppermute(head, axis, [((i + 1) % count, i) for i in range(ends)])  10.6 us
    all_to_all x1, blocking collectives, exchange_in_pieces(): lax.all_to_all(piece, axis, split_axis=0, concat_axis=0, tiled=True)  9.06 us
    ppermute x1, waiting for transfers between devices, with_halo(): lax.ppermute(tail, axis, [(i, (i + 1) % count) for i in range(ends)])  8.44 us
    all_to_all x1, waiting for transfers between devices, exchange_in_pieces(): lax.all_to_all(piece, axis, split_axis=0, concat_axis=0, tiled=True)  6.77 us
    all_to_all x1, blocking collectives, from_everyone(): lax.all_to_all(jnp.broadcast_to(x[None], (size, *x.shape)), axis, 0, 0, t...  5.42 us
    reduce_sum x3, other arithmetic, balance(): jnp.sum(kernel * row_weight, axis=1, keepdims=True) + filler  4.12 us
  transfers between devices with their start and end apart: 5, of which 4 were waited for; matrix products, arithmetic and copies ran while one was open for 2% of the time, Pallas kernels for 0%

commit v1 on v0

--- a/solution.py
+++ b/solution.py
@@ -116,7 +116,10 @@
     my_mask = lax.dynamic_slice_in_dim(mask_all, first, share, 0)
     full_time = gather_directly(subject_data, "tm", 3)
     extended = with_halo(full_time, (("slab", 1),), blocks_here)
-    mine = lax.all_to_all(template, "tm", split_axis=0, concat_axis=2, tiled=True)
+    peers = lax.axis_size("tm")
+    parts = jnp.stack(jnp.split(template, peers, axis=0), axis=0)
+    parts = lax.all_to_all(parts, "tm", split_axis=0, concat_axis=0)
+    mine = jnp.concatenate(parts, axis=2)
     col_norm = lax.rsqrt(square_sum(extended) + 1e-06)
     row_norm = lax.rsqrt(square_sum(mine) + 1e-06)
 

time: 118 us -> 118 us (level)
  transfers between devices with their start and end apart: 5 -> 5, of which waited for: 4 -> 4; matrix products, arithmetic and copies ran while one was open for 2% -> 3% of each run, Pallas kernels for 0% -> 0%
where the time goes in v1:
time: 118 us; the launch traced here: 117 us
  waiting for transfers between devices  46.3 us (39%)
  starting transfers between devices  23.5 us (20%)
  other arithmetic  16.4 us (14%)
  blocking collectives  14.5 us (12%)
  local copies, waits for them, and re-layouts  8.37 us (7%)
  matrix products  7.33 us (6%)
    ppermute x1, waiting for transfers between devices, with_halo(): lax.ppermute(head, axis, [((i + 1) % count, i) for i in range(ends)])  16.6 us
    all_to_all x1, waiting for transfers between devices, from_everyone(): lax.all_to_all(jnp.broadcast_to(x[None], (size, *x.shape)), axis, 0, 0, t...  14.5 us
    ppermute x1, starting transfers between devices, with_halo(): lax.ppermute(head, axis, [((i + 1) % count, i) for i in range(ends)])  10.6 us
    all_to_all x1, blocking collectives, exchange_in_pieces(): lax.all_to_all(piece, axis, split_axis=0, concat_axis=0, tiled=True)  9.06 us
    ppermute x1, waiting for transfers between devices, with_halo(): lax.ppermute(tail, axis, [(i, (i + 1) % count) for i in range(ends)])  8.44 us
    all_to_all x1, waiting for transfers between devices, exchange_in_pieces(): lax.all_to_all(piece, axis, split_axis=0, concat_axis=0, tiled=True)  6.77 us
    all_to_all x1, blocking collectives, from_everyone(): lax.all_to_all(jnp.broadcast_to(x[None], (size, *x.shape)), axis, 0, 0, t...  5.42 us
    reduce_sum x3, other arithmetic, balance(): jnp.sum(kernel * row_weight, axis=1, keepdims=True) + filler  4.12 us
  transfers between devices with their start and end apart: 5, of which 4 were waited for; matrix products, arithmetic and copies ran while one was open for 3% of the time, Pallas kernels for 0%

profile of v1, /device:TPU:2, one launch (start us, length us, event | category | flops | bytes accessed | tf_op | source)
XLA Modules:
  0.0 117.3 jit_solution(8858030117045173728)
XLA Ops:
  0.0 2.2 %broadcast_in_dim.73 = bf16[2,1,2,128,1024]{4,3,2,1,0:T(8,128)(2,1)} broadcast(bf16[2,128,1024]{2,1,0:T(8,128)(2,1)} %bitcast.119), dimensions={2,3,4} | broadcast | bytes 1572864 | tf_op jit(solution)/shard_map/broadcast_in_dim | solution.py:11
  2.2 3.6 %all-to-all-start = ((bf16[2,1,2,128,1024]{4,3,2,1,0:T(8,128)(2,1)}), bf16[2,1,2,128,1024]{4,3,2,1,0:T(8,128)(2,1)S(1)}, u32[]{:S(2)}, u32[]{:S(2)}) async-start(bf16[2,1,2,128,1024]{4,3,2,1,0:T(8,128)(2,1)} %broadcast_in_dim.73), calls=%async_computation | async-start | bytes 2097152 | tf_op jit(solution)/shard_map/all_to_all | solution.py:11
  5.9 0.8 pad_maximum_fusion
  6.7 14.5 %all-to-all-done = bf16[2,1,2,128,1024]{4,3,2,1,0:T(8,128)(2,1)S(1)} async-done(((bf16[2,1,2,128,1024]{4,3,2,1,0:T(8,128)(2,1)}), bf16[2,1,2,128,1024]{4,3,2,1,0:T(8,128)(2,1)S(1)}, u32[]{:S(2)}, u32[]{:S(2)}) %all-to-all-start) | async-done | bytes 1048608 | tf_op jit(solution)/shard_map/all_to_all | solution.py:11
  21.2 3.5 %all-to-all-start.1 = ((bf16[2,1,128,1024]{3,2,1,0:T(8,128)(2,1)}), bf16[2,1,128,1024]{3,2,1,0:T(8,128)(2,1)S(1)}, u32[]{:S(2)}, u32[]{:S(2)}) async-start(bf16[2,1,128,1024]{3,2,1,0:T(8,128)(2,1)} %pad_maximum_fusion), calls=%async_computation.1 | async-start | bytes 1048576 | tf_op jit(solution)/shard_map/all_to_all | solution.py:121
  24.7 0.1 copy.37
  24.8 10.6 %collective-permute-start.1 = (bf16[1,2,128,2048]{3,2,1,0:T(8,128)(2,1)S(1)}, bf16[1,2,128,2048]{3,2,1,0:T(8,128)(2,1)}, u32[]{:S(2)}, u32[]{:S(2)}) collective-permute-start(bf16[1,2,128,2048]{3,2,1,0:T(8,128)(2,1)S(1)} %bitcast.110), channel_id=1, source_target_pairs={{4,0},{8,4},{12,8},{16,12},{20,16},{24,20},{28,24},{32,28},{36,32}... | collective-permute-start | bytes 3145736 | tf_op jit(solution)/shard_map/ppermute | solution.py:39
  35.4 1.9 %collective-permute-start = (bf16[1,2,128,2048]{3,2,1,0:T(8,128)(2,1)S(1)}, bf16[1,2,128,2048]{3,2,1,0:T(8,128)(2,1)}, u32[]{:S(2)}, u32[]{:S(2)}) collective-permute-start(bf16[1,2,128,2048]{3,2,1,0:T(8,128)(2,1)S(1)} %bitcast.111), channel_id=1, source_target_pairs={{0,4},{4,8},{8,12},{12,16},{16,20},{20,24},{24,28},{28,32},{32,36}... | collective-permute-start | bytes 3145736 | tf_op jit(solution)/shard_map/ppermute | solution.py:37
  37.4 0.6 fusion.24
  38.7 0.0 all-to-all-done.1
  38.7 0.5 copy.22
  39.3 0.4 reshape.369
  39.6 0.1 copy.38
  39.8 0.2 fusion.15
  40.0 16.6 %collective-permute-done.1 = bf16[1,2,128,2048]{3,2,1,0:T(8,128)(2,1)} collective-permute-done((bf16[1,2,128,2048]{3,2,1,0:T(8,128)(2,1)S(1)}, bf16[1,2,128,2048]{3,2,1,0:T(8,128)(2,1)}, u32[]{:S(2)}, u32[]{:S(2)}) %collective-permute-start.1) | collective-permute-done | bytes 1048608 | tf_op jit(solution)/shard_map/ppermute | solution.py:39
  56.6 8.4 %collective-permute-done = bf16[1,2,128,2048]{3,2,1,0:T(8,128)(2,1)} collective-permute-done((bf16[1,2,128,2048]{3,2,1,0:T(8,128)(2,1)S(1)}, bf16[1,2,128,2048]{3,2,1,0:T(8,128)(2,1)}, u32[]{:S(2)}, u32[]{:S(2)}) %collective-permute-start) | collective-permute-done | bytes 1048608 | tf_op jit(solution)/shard_map/ppermute | solution.py:37
  65.0 2.0 %fusion = f32[6,128]{1,0:T(8,128)S(1)} fusion(bf16[1,2,128,2048]{3,2,1,0:T(8,128)(2,1)} %collective-permute-done.1, bf16[1,2,128,2048]{3,2,1,0:T(8,128)(2,1)S(1)} %bitcast.112, bf16[1,2,128,2048]{3,2,1,0:T(8,128)(2,1)} %collective-permute-done), kind=kLoop, calls=%fused_computation.3 | loop fusion | flops 7863552 | bytes 3148800 | tf_op jit(solution)/shard_map/...t,...t->.../dot_general | solution.py:82
  67.0 0.6 gather_fusion.1
  67.6 2.5 %convolution_bitcast_fusion.3 = f32[128,6,128]{0,2,1:T(8,128)S(1)} fusion(bf16[128,2048,1]{1,0,2:T(8,128)(2,1)S(1)} %reshape.369, bf16[1,2,128,2048]{3,2,1,0:T(8,128)(2,1)} %collective-permute-done.1, bf16[1,2,128,2048]{3,2,1,0:T(8,128)(2,1)S(1)} %bitcast.113, bf16[1,2,128,2048]{3,2,1,0:T(8,128)(2,1)} %collective-permute-done), kind=kOutput, calls=%fused_computation.30 | convolution fusion | flops 405798912 | bytes 4063232 | tf_op jit(solution)/shard_map/while/body/eval_jaxpr/it,sejt->siej/dot_general | solution.py:86
  70.1 0.7 gather_fusion
  70.8 0.1 broadcast_select_fusion
  70.9 0.8 fusion.26
  71.7 1.4 %multiply_reduce_fusion.5 = f32[27,128]{1,0:T(8,128)S(1)} fusion(f32[128]{0:T(128)S(1)} %broadcast_divide_fusion.2, f32[27]{0:T(128)S(1)} %get-tuple-element.20, f32[27,128]{1,0:T(8,128)S(1)} %broadcast_select_fusion, f32[128]{0:T(128)S(1)} %add_rsqrt_fusion.1, f32[27,128,128]{1,2,0:T(8,128)S(1)} %gather_fusion, pred[27]{0:T(512)(128)(4,1)S(1)} %get-tuple-element.21), kind=kLoop, calls=%fused_computation.27 | loop fusion | flops 3093120 | bytes 1798279 | tf_op jit(solution)/shard_map/while/body/eval_jaxpr/reduce_sum | solution.py:76
  73.1 0.1 add_divide_fusion.2
  73.1 1.3 %multiply_reduce_fusion.4 = f32[128]{0:T(128)S(1)} fusion(f32[27,128]{1,0:T(8,128)S(1)} %add_divide_fusion.2, f32[27]{0:T(128)S(1)} %get-tuple-element.20, f32[27,128]{1,0:T(8,128)S(1)} %broadcast_select_fusion, f32[128]{0:T(128)S(1)} %add_rsqrt_fusion.1, f32[27,128,128]{1,2,0:T(8,128)S(1)} %gather_fusion, pred[27]{0:T(512)(128)(4,1)S(1)} %get-tuple-element.21), kind=kLoop, calls=%fused_computation.26 | loop fusion | flops 3096448 | bytes 1798279 | tf_op jit(solution)/shard_map/while/body/eval_jaxpr/reduce_sum | solution.py:75
  74.5 1.4 %multiply_reduce_fusion.3 = f32[27,128]{1,0:T(8,128)S(1)} fusion(f32[128]{0:T(128)S(1)} %broadcast_divide_fusion.1, f32[27]{0:T(128)S(1)} %get-tuple-element.20, f32[27,128]{1,0:T(8,128)S(1)} %broadcast_select_fusion, f32[128]{0:T(128)S(1)} %add_rsqrt_fusion.1, f32[27,128,128]{1,2,0:T(8,128)S(1)} %gather_fusion, pred[27]{0:T(512)(128)(4,1)S(1)} %get-tuple-element.21), kind=kLoop, calls=%fused_computation.25 | loop fusion | flops 3093120 | bytes 1798279 | tf_op jit(solution)/shard_map/while/body/eval_jaxpr/reduce_sum | solution.py:76
  75.9 0.1 add_divide_fusion.1
  76.0 1.3 %multiply_reduce_fusion.2 = f32[128]{0:T(128)S(1)} fusion(f32[27,128]{1,0:T(8,128)S(1)} %add_divide_fusion.1, f32[27]{0:T(128)S(1)} %get-tuple-element.20, f32[27,128]{1,0:T(8,128)S(1)} %broadcast_select_fusion, f32[128]{0:T(128)S(1)} %add_rsqrt_fusion.1, f32[27,128,128]{1,2,0:T(8,128)S(1)} %gather_fusion, pred[27]{0:T(512)(128)(4,1)S(1)} %get-tuple-element.21), kind=kLoop, calls=%fused_computation.24 | loop fusion | flops 3096448 | bytes 1798279 | tf_op jit(solution)/shard_map/while/body/eval_jaxpr/reduce_sum | solution.py:75
  77.3 1.4 %multiply_reduce_fusion.1 = f32[27,128]{1,0:T(8,128)S(1)} fusion(f32[128]{0:T(128)S(1)} %broadcast_divide_fusion, f32[27]{0:T(128)S(1)} %get-tuple-element.20, f32[27,128]{1,0:T(8,128)S(1)} %broadcast_select_fusion, f32[128]{0:T(128)S(1)} %add_rsqrt_fusion.1, f32[27,128,128]{1,2,0:T(8,128)S(1)} %gather_fusion, pred[27]{0:T(512)(128)(4,1)S(1)} %get-tuple-element.21), kind=kLoop, calls=%fused_computation.23 | loop fusion | flops 3093120 | bytes 1798279 | tf_op jit(solution)/shard_map/while/body/eval_jaxpr/reduce_sum | solution.py:76
  78.7 0.1 add_divide_fusion
  78.8 1.3 %multiply_reduce_fusion = f32[128]{0:T(128)S(1)} fusion(f32[27,128]{1,0:T(8,128)S(1)} %add_divide_fusion, f32[27]{0:T(128)S(1)} %get-tuple-element.20, f32[27,128]{1,0:T(8,128)S(1)} %broadcast_select_fusion, f32[128]{0:T(128)S(1)} %add_rsqrt_fusion.1, f32[27,128,128]{1,2,0:T(8,128)S(1)} %gather_fusion, pred[27]{0:T(512)(128)(4,1)S(1)} %get-tuple-element.21), kind=kLoop, calls=%fused_computation.22 | loop fusion | flops 3096448 | bytes 1798279 | tf_op jit(solution)/shard_map/while/body/eval_jaxpr/reduce_sum | solution.py:78
  80.1 2.3 %fusion.14 = bf16[128,27,128]{0,2,1:T(8,128)(2,1)} fusion(f32[27,128,128]{1,2,0:T(8,128)S(1)} %gather_fusion, f32[128]{0:T(128)S(1)} %multiply_reduce_fusion, f32[27,128]{1,0:T(8,128)S(1)} %add_divide_fusion, f32[27]{0:T(128)S(1)} %get-tuple-element.20, f32[27,128]{1,0:T(8,128)S(1)} %broadcast_select_fusion, f32[128]{0:T(128)S(1)} %add_rsqrt_fusion.1, ...), kind=kLoop, calls=%fused_computation.28 | loop fusion | flops 3538944 | bytes 2683015 | tf_op jit(solution)/shard_map/while/body/eval_jaxpr/convert_element_type | solution.py:78
  82.4 1.9 %copy.23 = bf16[128,27,128]{2,1,0:T(8,128)(2,1)S(1)} copy(bf16[128,27,128]{0,2,1:T(8,128)(2,1)} %fusion.14) | data formatting | bytes 1769472 | tf_op jit(solution)/shard_map/while/body/eval_jaxpr/convert_element_type | solution.py:78
  84.4 0.3 convert_bitcast_fusion
  84.6 2.3 %convolution_bitcast_fusion = f32[128,2048]{1,0:T(8,128)S(1)} fusion(bf16[128,6,128]{2,1,0:T(8,128)(2,1)S(1)} %get-tuple-element.36, bf16[1,2,128,2048]{3,2,1,0:T(8,128)(2,1)} %collective-permute-done.1, bf16[1,2,128,2048]{3,2,1,0:T(8,128)(2,1)S(1)} %bitcast.114, bf16[1,2,128,2048]{3,2,1,0:T(8,128)(2,1)} %collective-permute-done), kind=kOutput, calls=%fused_computation.5 | convolution fusion | flops 405798912 | bytes 4390912 | tf_op jit(solution)/shard_map/while/body/eval_jaxpr/siej,sejt->it/dot_general | solution.py:100
  86.9 2.3 %fusion.1 = f32[128,2048]{1,0:T(8,128)S(1)} fusion(f32[128,2048]{1,0:T(8,128)S(1)} %convolution_bitcast_fusion, bf16[128,6,128]{2,1,0:T(8,128)(2,1)S(1)} %get-tuple-element.34, bf16[1,2,128,2048]{3,2,1,0:T(8,128)(2,1)} %collective-permute-done.1, bf16[1,2,128,2048]{3,2,1,0:T(8,128)(2,1)S(1)} %bitcast.115, bf16[1,2,128,2048]{3,2,1,0:T(8,128)(2,1)} %collective-permute-done), kind=kOutput, calls=%fused_computation.7 | convolution fusion | flops 406061056 | bytes 5439488 | tf_op jit(solution)/shard_map/while/body/eval_jaxpr/siej,sejt->it/dot_general | solution.py:99
  89.2 0.2 broadcast_in_dim.79
  89.5 5.4 %all_to_all.25 = f32[2,1,128,2048]{3,2,1,0:T(8,128)S(1)} all-to-all(f32[2,1,128,2048]{3,2,1,0:T(8,128)S(1)} %broadcast_in_dim.79), channel_id=1, replica_groups=mesh['slab'=64,'subj'=2,'tm'=2] {'subj'}, dimensions={0} | all-to-all | bytes 4194304 | tf_op jit(solution)/shard_map/all_to_all | solution.py:11
  94.9 0.2 reduce_sum.97
  95.1 0.1 multiply_convert_fusion
  95.2 0.3 copy.26
  95.5 0.2 fusion.29
  95.7 0.9 copy.27
  96.6 3.9 %all-to-all-start.3 = ((bf16[2,1,64,1024]{3,2,1,0:T(8,128)(2,1)}), bf16[2,1,64,1024]{3,2,1,0:T(8,128)(2,1)S(1)}, u32[]{:S(2)}, u32[]{:S(2)}) async-start(bf16[2,1,64,1024]{3,2,1,0:T(8,128)(2,1)} %copy.27), calls=%async_computation.3 | async-start | bytes 524288 | tf_op jit(solution)/shard_map/all_to_all | solution.py:62
  100.5 0.2 copy.28
  100.7 6.8 %all-to-all-done.3 = bf16[2,1,64,1024]{3,2,1,0:T(8,128)(2,1)S(1)} async-done(((bf16[2,1,64,1024]{3,2,1,0:T(8,128)(2,1)}), bf16[2,1,64,1024]{3,2,1,0:T(8,128)(2,1)S(1)}, u32[]{:S(2)}, u32[]{:S(2)}) %all-to-all-start.3) | async-done | bytes 262176 | tf_op jit(solution)/shard_map/all_to_all | solution.py:62
  107.4 9.1 %all_to_all.26 = bf16[2,1,64,1024]{3,2,1,0:T(8,128)(2,1)S(1)} all-to-all(bf16[2,1,64,1024]{3,2,1,0:T(8,128)(2,1)S(1)} %copy.28), channel_id=1, replica_groups=mesh['slab'=64,'subj'=2,'tm'=2] {'tm'}, dimensions={0} | all-to-all | bytes 524288 | tf_op jit(solution)/shard_map/all_to_all | solution.py:62
  116.5 0.8 maximum_bitcast_fusion.1
  (19 shorter events, 0.1 us)
Async XLA Ops:
  0.0 5.8 %copy-start = (bf16[2,128,1024]{2,1,0:T(8,128)(2,1)S(1)}, bf16[2,128,1024]{2,1,0:T(8,128)(2,1)}, u32[]{:S(2)}) copy-start(bf16[2,128,1024]{2,1,0:T(8,128)(2,1)} %param.5) | copy-start | bytes 1572868
  2.2 18.9 %all-to-all-start = ((bf16[2,1,2,128,1024]{4,3,2,1,0:T(8,128)(2,1)}), bf16[2,1,2,128,1024]{4,3,2,1,0:T(8,128)(2,1)S(1)}, u32[]{:S(2)}, u32[]{:S(2)}) async-start(bf16[2,1,2,128,1024]{4,3,2,1,0:T(8,128)(2,1)} %broadcast_in_dim.73), calls=%async_computation | async-start | bytes 2097152 | tf_op jit(solution)/shard_map/all_to_all | solution.py:11
  6.7 30.6 %copy-start.1 = (s32[2,27]{1,0:T(2,128)S(1)}, s32[2,27]{1,0:T(2,128)}, u32[]{:S(2)}) copy-start(s32[2,27]{1,0:T(2,128)} %param.6) | copy-start | bytes 652
  6.7 30.6 %copy-start.2 = (s32[2,27]{1,0:T(2,128)S(1)}, s32[2,27]{1,0:T(2,128)}, u32[]{:S(2)}) copy-start(s32[2,27]{1,0:T(2,128)} %param.7) | copy-start | bytes 652
  21.2 17.5 %all-to-all-start.1 = ((bf16[2,1,128,1024]{3,2,1,0:T(8,128)(2,1)}), bf16[2,1,128,1024]{3,2,1,0:T(8,128)(2,1)S(1)}, u32[]{:S(2)}, u32[]{:S(2)}) async-start(bf16[2,1,128,1024]{3,2,1,0:T(8,128)(2,1)} %pad_maximum_fusion), calls=%async_computation.1 | async-start | bytes 1048576 | tf_op jit(solution)/shard_map/all_to_all | solution.py:121
  24.8 31.8 %collective-permute-start.1 = (bf16[1,2,128,2048]{3,2,1,0:T(8,128)(2,1)S(1)}, bf16[1,2,128,2048]{3,2,1,0:T(8,128)(2,1)}, u32[]{:S(2)}, u32[]{:S(2)}) collective-permute-start(bf16[1,2,128,2048]{3,2,1,0:T(8,128)(2,1)S(1)} %bitcast.110), channel_id=1, source_target_pairs={{4,0},{8,4},{12,8},{16,12},{20,16},{24,20},{28,24},{32,28},{36,32}... | collective-permute-start | bytes 3145736 | tf_op jit(solution)/shard_map/ppermute | solution.py:39
  35.4 29.6 %collective-permute-start = (bf16[1,2,128,2048]{3,2,1,0:T(8,128)(2,1)S(1)}, bf16[1,2,128,2048]{3,2,1,0:T(8,128)(2,1)}, u32[]{:S(2)}, u32[]{:S(2)}) collective-permute-start(bf16[1,2,128,2048]{3,2,1,0:T(8,128)(2,1)S(1)} %bitcast.111), channel_id=1, source_target_pairs={{0,4},{4,8},{8,12},{12,16},{16,20},{20,24},{24,28},{28,32},{32,36}... | collective-permute-start | bytes 3145736 | tf_op jit(solution)/shard_map/ppermute | solution.py:37
  96.6 10.9 %all-to-all-start.3 = ((bf16[2,1,64,1024]{3,2,1,0:T(8,128)(2,1)}), bf16[2,1,64,1024]{3,2,1,0:T(8,128)(2,1)S(1)}, u32[]{:S(2)}, u32[]{:S(2)}) async-start(bf16[2,1,64,1024]{3,2,1,0:T(8,128)(2,1)} %copy.27), calls=%async_computation.3 | async-start | bytes 524288 | tf_op jit(solution)/shard_map/all_to_all | solution.py:62
